TPU v7x, 32 devices: a whole 2x2x4 slice. The times are simulated.
32 devices in a mesh: wave: 4 (over x, core), dom: 8 (over z, y).
Axes of the slice: x: 2, y: 2, z: 4, core: 2. Of those that a mesh axis runs over, the one named last changes fastest.
Arguments:
- rhs: float32 [4, 8, 12, 32, 625], P('wave', 'dom'), may hold values from -6 to 6
- start: float32 [4, 8, 12, 32, 625], P('wave', 'dom'), may hold values from -6 to 6
- block_inv: bfloat16 [4, 8, 12, 625, 625], P('wave', 'dom'), as said below
- coup_up: bfloat16 [4, 8, 12, 3, 128, 625], P('wave', 'dom'), may hold values from -0.21875 to 0.21875
- coup_down: bfloat16 [4, 8, 12, 3, 128, 625], P('wave', 'dom'), may hold values from -0.21875 to 0.21875
- down_pick: int32 [4, 8, 8, 9], P('wave', 'dom'), may hold values from 0 to 36, as said below
- down_slot: int32 [4, 8, 36], P('wave', 'dom'), may hold values from 0 to 72, as said below
- up_pick: int32 [4, 8, 8, 9], P('wave', 'dom'), may hold values from 0 to 36, as said below
- up_slot: int32 [4, 8, 36], P('wave', 'dom'), may hold values from 0 to 72, as said below
Outputs:
- half_sweep: float32 [4, 8, 12, 32, 625], P('wave', 'dom')
- solution: float32 [4, 8, 12, 32, 625], P('wave', 'dom')
Inputs may be any that keep to these rules, and one draw needn't show every extreme that they name: `block_inv`: each block is the inverse of an element's diagonal block. For l < 3, every down face of every partition s of level l appears exactly once among the used entries of down_pick[l, s]; the slots of a pair (s, d) are used from j = 0 up, and unused slots and all of level 3 hold 36. Every partition of a level below the last fills all 9 slots toward some partition. down_slot[l, d, f] = s * 9 + j names a used slot j of down_pick[l - 1, s, d]; each used slot is named by exactly one up face; level 0 holds 72. up_pick[l + 1, d, s, j] is the up face of partition d at level l + 1 joined to the down face down_pick[l, s, d, j]; unused slots and all of level 0 hold 36. up_slot[l, s, f] = d * 9 + j names a used slot j of up_pick[l + 1, d, s]; each used slot is named by exactly one down face; level 3 holds 72.
All inputs are finite; a program needn't handle non-finite values.
Results may differ from a plain program's by a relative error of at most 0.018.
Values may be sent and summed in bfloat16 or wider, within the bound.
A program may use at most 128 MiB of HBM per device.

v0:
```python
import jax
import jax.numpy as jnp
from jax import lax
from jax.sharding import PartitionSpec as P

VARS = 5
NODES1 = 5
FACE = 125
FTR = 128


def shifted(array, axis, by):
    peers = lax.axis_size(axis)
    pairs = [(i, i + by) for i in range(peers) if 0 <= i + by < peers]
    return lax.ppermute(array, axis, pairs)


def face_traces(field, face_side):
    lead_dims = field.shape[:-1]
    cube = field.reshape(lead_dims + (VARS, NODES1, NODES1, NODES1))
    edge_at = 0 if face_side == 0 else NODES1 - 1
    three_faces = [cube[..., edge_at, :, :], cube[..., :, edge_at, :], cube[..., :, :, edge_at]]
    flat_faces = [one_face.reshape(lead_dims + (FACE,)) for one_face in three_faces]
    stacked = jnp.stack(flat_faces, axis=-3)
    padding = [(0, 0)] * (stacked.ndim - 1) + [(0, FTR - FACE)]
    padded = jnp.pad(stacked, padding).astype(jnp.bfloat16)
    shape_now = padded.shape
    return padded.reshape(shape_now[:-4] + (shape_now[-4] * 3,) + shape_now[-2:])


def pack_faces(traces, pick_list):
    blank = jnp.zeros((1,) + traces.shape[1:], jnp.bfloat16)
    extended = jnp.concatenate([traces, blank], axis=0)
    return extended[pick_list]


def unpack_faces(received, slot_list):
    flat_rows = received.reshape((-1,) + received.shape[2:])
    blank = jnp.zeros((1,) + flat_rows.shape[1:], jnp.bfloat16)
    extended = jnp.concatenate([flat_rows, blank], axis=0)
    return extended[slot_list]


def couple_faces(neighbours, coupling):
    near_faces = neighbours.reshape(coupling.shape[0], 3, neighbours.shape[1], neighbours.shape[2])
    return jnp.einsum("ekrt,ektb->erb", near_faces, coupling, preferred_element_type=jnp.float32)


def route_down(buffer):
    spread = lax.all_to_all(buffer, "dom", split_axis=0, concat_axis=0, tiled=True)
    return shifted(spread, "wave", 1)


def route_up(buffer):
    spread = lax.all_to_all(buffer, "dom", split_axis=0, concat_axis=0, tiled=True)
    return shifted(spread, "wave", -1)


def run_sweep(
    state_init,
    rhs_local,
    first_near,
    first_coup,
    second_coup,
    second_slot,
    inverse,
    send_pick,
    send_side,
    router,
    sweep_rank,
    level_count,
    group_count,
    computes,
):
    rows_all = rhs_local.shape[1]
    settled = rhs_local - couple_faces(first_near, first_coup)
    holder_init = jnp.zeros((send_pick.shape[0], send_pick.shape[1], rows_all, FTR), jnp.bfloat16)

    def one_turn(turn_no, carry):
        field_now, holder = carry
        group_at = turn_no - sweep_rank
        active = (group_at >= 0) & (group_at < group_count) & computes

        def fresh_rows():
            chain_near = unpack_faces(holder, second_slot)
            residual = (settled - couple_faces(chain_near, second_coup)).astype(jnp.bfloat16)
            return jnp.einsum("eri,eij->erj", residual, inverse, preferred_element_type=jnp.float32)

        def stale_rows():
            return field_now

        new_rows = lax.cond(active, fresh_rows, stale_rows)
        field_now = new_rows
        arrived = router(pack_faces(face_traces(new_rows, send_side), send_pick))
        incoming_at = turn_no - sweep_rank + 1
        accept = (incoming_at >= 0) & (incoming_at < group_count)
        current = holder
        holder = jnp.where(accept, arrived, current)
        return (field_now, holder)

    return lax.fori_loop(0, level_count + group_count - 1, one_turn, (state_init, holder_init))


def local(rhs, start, block_inv, coup_up, coup_down, down_pick, down_slot, up_pick, up_slot):
    rhs_local = rhs[0, 0]
    start_local = start[0, 0]
    inverse = block_inv[0, 0]
    coupling_up = coup_up[0, 0]
    coupling_down = coup_down[0, 0]
    pick_down = down_pick[0, 0]
    slot_down = down_slot[0, 0]
    pick_up = up_pick[0, 0]
    slot_up = up_slot[0, 0]
    level_count = lax.axis_size("wave")
    wave_rank = lax.axis_index("wave")
    group_count = 1
    lower_old = unpack_faces(route_up(pack_faces(face_traces(start_local, 0), pick_up)), slot_up)
    half_state, holder_forward = run_sweep(
        start_local,
        rhs_local,
        lower_old,
        coupling_down,
        coupling_up,
        slot_down,
        inverse,
        pick_down,
        1,
        route_down,
        wave_rank,
        level_count,
        group_count,
        jnp.bool_(True),
    )
    upper_new = unpack_faces(holder_forward, slot_down)
    back_rank = level_count - 1 - wave_rank
    final_state, leftover = run_sweep(
        half_state,
        rhs_local,
        upper_new,
        coupling_up,
        coupling_down,
        slot_up,
        inverse,
        pick_up,
        0,
        route_up,
        back_rank,
        level_count,
        group_count,
        back_rank >= 1,
    )
    return (half_state[None, None], final_state[None, None])


def solution(mesh):
    placed = (
        P("wave", "dom", None, None, None),
        P("wave", "dom", None, None, None),
        P("wave", "dom", None, None, None),
        P("wave", "dom", None, None, None, None),
        P("wave", "dom", None, None, None, None),
        P("wave", "dom", None, None),
        P("wave", "dom", None),
        P("wave", "dom", None, None),
        P("wave", "dom", None),
    )
    return jax.shard_map(
        local,
        mesh=mesh,
        in_specs=placed,
        out_specs=(P("wave", "dom", None, None, None), P("wave", "dom", None, None, None)),
        check_vma=False,
    )
```

profile of v0, /device:TPU:0, one launch (start us, length us, event | category | flops | bytes accessed | tf_op | source)
XLA Modules:
  0.0 421.9 jit_solution(1882159246736688270)
XLA Ops:
  2.9 5.4 %copy.33 = bf16[1,1,12,32,625]{3,2,4,1,0:T(8,128)(2,1)S(1)} copy(f32[1,1,12,32,625]{4,3,2,1,0:T(8,128)} %copy.80) | data formatting | bytes 1440000 | tf_op args[1]
  16.7 7.4 %all-to-all-start.2 = ((bf16[8,9,32,128]{3,2,1,0:T(8,128)(2,1)}), bf16[8,9,32,128]{3,2,1,0:T(8,128)(2,1)S(1)}, u32[]{:S(2)}, u32[]{:S(2)}) async-start(bf16[8,9,32,128]{3,2,1,0:T(8,128)(2,1)} %bitcast.18), calls=%async_computation.2 | async-start | bytes 1179648 | tf_op jit(solution)/shard_map/all_to_all | solution.py:55
  24.2 15.9 %all-to-all-done.2 = bf16[8,9,32,128]{3,2,1,0:T(8,128)(2,1)S(1)} async-done(((bf16[8,9,32,128]{3,2,1,0:T(8,128)(2,1)}), bf16[8,9,32,128]{3,2,1,0:T(8,128)(2,1)S(1)}, u32[]{:S(2)}, u32[]{:S(2)}) %all-to-all-start.2) | async-done | bytes 589856 | tf_op jit(solution)/shard_map/all_to_all | solution.py:55
  44.6 5.6 %fusion.17 = f32[12,32,625]{2,1,0:T(8,128)} fusion(bf16[12,3,32,128]{3,2,1,0:T(8,128)(2,1)S(1)} %bitcast.158, f32[1,1,12,32,625]{4,3,2,1,0:T(8,128)S(1)} %copy-done, bf16[1,1,12,3,128,625]{4,5,3,2,1,0:T(8,128)(2,1)} %param.21), kind=kOutput, calls=%fused_computation.42 | convolution fusion | flops 184560000 | bytes 7974912 | tf_op jit(solution)/shard_map/ekrt,ektb->erb/dot_general | solution.py:46
  50.2 173.7 %while.42 = (s32[]{:T(128)}, f32[12,32,625]{2,1,0:T(8,128)}, bf16[8,9,32,128]{3,2,1,0:T(8,128)(2,1)S(1)}, s32[]{:T(128)}, s32[36]{0:T(128)}, /*index=5*/bf16[12,...) while((s32[]{:T(128)}, f32[12,32,625]{2,1,0:T(8,128)}, ...), condition=%wide.region_3.4_spmd.clone, body=%wide.region_0.3_spmd.clone.sunk | while | flops 487161664 | bytes 30579004 | solution.py:101
  50.2 11.5 %conditional.6 = (f32[12,32,625]{2,1,0:T(8,128)}) conditional(s32[]{:T(128)} %convert_element_type.69, f32[12,32,625]{2,1,0:T(8,128)} %get-tuple-element.750, (bf16[8,9,32,128]{3,2,1,0:T(8,128)(2,1)S(1)}, s32[36]{0:T(128)}, bf16[12,3,128,625]{2,3,1,0:T(8,128)(2,1)}, f32[12,32,625]{2,1,0:T(8,128)}, bf16[12,625,625]{2,1,0:T(8,128)(2,1)}) %tuple.108), branch_computations={%region_1.1_spmd, %region_2.2_spmd} | conditional | flops 484801120 | bytes 19132258 | solution.py:92
  51.6 10.2 %fusion.2 = f32[12,32,625]{2,1,0:T(8,128)} fusion(bf16[12,625,625]{2,1,0:T(8,128)(2,1)} %get-tuple-element.485, f32[12,32,625]{2,1,0:T(8,128)} %get-tuple-element.481, bf16[12,3,32,128]{3,2,1,0:T(8,128)(2,1)S(1)} %bitcast.150, bf16[12,3,128,625]{2,3,1,0:T(8,128)(2,1)} %get-tuple-element.484), kind=kOutput, calls=%fused_computation.10 | convolution fusion | flops 484800000 | bytes 17349912 | tf_op jit(solution)/shard_map/while/body/eval_jaxpr/cond/branch_1_fun/eri,eij->erj/dot_general | solution.py:87
  61.7 5.4 %copy.49 = bf16[12,32,625]{1,0,2:T(8,128)(2,1)S(1)} copy(f32[12,32,625]{2,1,0:T(8,128)} %get-tuple-element.812) | data formatting | bytes 1440000 | tf_op jit(solution)/shard_map/while/body/eval_jaxpr/cond | solution.py:92
  74.8 16.0 %all_to_all.33 = bf16[8,9,32,128]{3,2,1,0:T(8,128)(2,1)S(1)} all-to-all(bf16[8,9,32,128]{3,2,1,0:T(8,128)(2,1)S(1)} %bitcast.140), channel_id=1, replica_groups=mesh['wave'=4,'dom'=8] {'dom'}, dimensions={0} | all-to-all | bytes 1179648 | tf_op jit(solution)/shard_map/while/body/eval_jaxpr/all_to_all | solution.py:50
  93.8 5.4 %copy.49 = bf16[12,32,625]{1,0,2:T(8,128)(2,1)S(1)} copy(f32[12,32,625]{2,1,0:T(8,128)} %get-tuple-element.812) | data formatting | bytes 1440000 | tf_op jit(solution)/shard_map/while/body/eval_jaxpr/cond | solution.py:92
  106.9 14.4 %all_to_all.33 = bf16[8,9,32,128]{3,2,1,0:T(8,128)(2,1)S(1)} all-to-all(bf16[8,9,32,128]{3,2,1,0:T(8,128)(2,1)S(1)} %bitcast.140), channel_id=1, replica_groups=mesh['wave'=4,'dom'=8] {'dom'}, dimensions={0} | all-to-all | bytes 1179648 | tf_op jit(solution)/shard_map/while/body/eval_jaxpr/all_to_all | solution.py:50
  121.3 15.6 %collective-permute-start = (bf16[8,9,32,128]{3,2,1,0:T(8,128)(2,1)S(1)}, bf16[8,9,32,128]{3,2,1,0:T(8,128)(2,1)S(1)}, u32[]{:S(2)}, u32[]{:S(2)}) collective-permute-start(bf16[8,9,32,128]{3,2,1,0:T(8,128)(2,1)S(1)} %all_to_all.33), channel_id=1, source_target_pairs={{0,8},{8,16},{16,24},{1,9},{9,17},{17,25},{2,10},{10,18},{18,26},{... | collective-permute-start | bytes 1769480 | tf_op jit(solution)/shard_map/while/body/eval_jaxpr/ppermute | solution.py:15
  138.7 5.4 %copy.49 = bf16[12,32,625]{1,0,2:T(8,128)(2,1)S(1)} copy(f32[12,32,625]{2,1,0:T(8,128)} %get-tuple-element.812) | data formatting | bytes 1440000 | tf_op jit(solution)/shard_map/while/body/eval_jaxpr/cond | solution.py:92
  151.7 17.9 %all_to_all.33 = bf16[8,9,32,128]{3,2,1,0:T(8,128)(2,1)S(1)} all-to-all(bf16[8,9,32,128]{3,2,1,0:T(8,128)(2,1)S(1)} %bitcast.140), channel_id=1, replica_groups=mesh['wave'=4,'dom'=8] {'dom'}, dimensions={0} | all-to-all | bytes 1179648 | tf_op jit(solution)/shard_map/while/body/eval_jaxpr/all_to_all | solution.py:50
  176.0 5.4 %copy.49 = bf16[12,32,625]{1,0,2:T(8,128)(2,1)S(1)} copy(f32[12,32,625]{2,1,0:T(8,128)} %get-tuple-element.812) | data formatting | bytes 1440000 | tf_op jit(solution)/shard_map/while/body/eval_jaxpr/cond | solution.py:92
  189.0 14.4 %all_to_all.33 = bf16[8,9,32,128]{3,2,1,0:T(8,128)(2,1)S(1)} all-to-all(bf16[8,9,32,128]{3,2,1,0:T(8,128)(2,1)S(1)} %bitcast.140), channel_id=1, replica_groups=mesh['wave'=4,'dom'=8] {'dom'}, dimensions={0} | all-to-all | bytes 1179648 | tf_op jit(solution)/shard_map/while/body/eval_jaxpr/all_to_all | solution.py:50
  203.5 18.7 %collective-permute-start = (bf16[8,9,32,128]{3,2,1,0:T(8,128)(2,1)S(1)}, bf16[8,9,32,128]{3,2,1,0:T(8,128)(2,1)S(1)}, u32[]{:S(2)}, u32[]{:S(2)}) collective-permute-start(bf16[8,9,32,128]{3,2,1,0:T(8,128)(2,1)S(1)} %all_to_all.33), channel_id=1, source_target_pairs={{0,8},{8,16},{16,24},{1,9},{9,17},{17,25},{2,10},{10,18},{18,26},{... | collective-permute-start | bytes 1769480 | tf_op jit(solution)/shard_map/while/body/eval_jaxpr/ppermute | solution.py:15
  226.8 5.8 %fusion.16 = f32[12,32,625]{2,1,0:T(8,128)} fusion(bf16[12,3,32,128]{3,2,1,0:T(8,128)(2,1)S(1)} %bitcast.159, f32[1,1,12,32,625]{4,3,2,1,0:T(8,128)} %param.17, bf16[1,1,12,3,128,625]{4,5,3,2,1,0:T(8,128)(2,1)} %bitcast.129), kind=kOutput, calls=%fused_computation.40 | convolution fusion | flops 184560000 | bytes 7974912 | tf_op jit(solution)/shard_map/ekrt,ektb->erb/dot_general | solution.py:46
  232.6 189.3 %while.43 = (s32[]{:T(128)}, f32[12,32,625]{2,1,0:T(8,128)}, bf16[8,9,32,128]{3,2,1,0:T(8,128)(2,1)}, s32[]{:T(128)}, pred[]{:T(512)}, /*index=5*/s32[36]{0:T(12...) while((s32[]{:T(128)}, f32[12,32,625]{2,1,0:T(8,128)}, ...), condition=%wide.region_7.8_spmd.clone, body=%wide.region_4.7_spmd.clone.sunk | while | flops 487161664 | bytes 30579016 | solution.py:101
  232.7 5.4 %copy.53 = bf16[12,32,625]{1,0,2:T(8,128)(2,1)S(1)} copy(f32[12,32,625]{2,1,0:T(8,128)} %get-tuple-element.813) | data formatting | bytes 1440000 | tf_op jit(solution)/shard_map/while/body/eval_jaxpr/cond | solution.py:92
  243.9 14.4 %all_to_all.34 = bf16[8,9,32,128]{3,2,1,0:T(8,128)(2,1)S(1)} all-to-all(bf16[8,9,32,128]{3,2,1,0:T(8,128)(2,1)S(1)} %bitcast.141), channel_id=1, replica_groups=mesh['wave'=4,'dom'=8] {'dom'}, dimensions={0} | all-to-all | bytes 1179648 | tf_op jit(solution)/shard_map/while/body/eval_jaxpr/all_to_all | solution.py:55
  259.6 15.3 %collective-permute-done.1 = bf16[8,9,32,128]{3,2,1,0:T(8,128)(2,1)S(1)} collective-permute-done((bf16[8,9,32,128]{3,2,1,0:T(8,128)(2,1)S(1)}, bf16[8,9,32,128]{3,2,1,0:T(8,128)(2,1)S(1)}, u32[]{:S(2)}, u32[]{:S(2)}) %collective-permute-start.1) | collective-permute-done | bytes 589856 | tf_op jit(solution)/shard_map/while/body/eval_jaxpr/ppermute | solution.py:15
  277.0 5.4 %copy.53 = bf16[12,32,625]{1,0,2:T(8,128)(2,1)S(1)} copy(f32[12,32,625]{2,1,0:T(8,128)} %get-tuple-element.813) | data formatting | bytes 1440000 | tf_op jit(solution)/shard_map/while/body/eval_jaxpr/cond | solution.py:92
  288.2 14.4 %all_to_all.34 = bf16[8,9,32,128]{3,2,1,0:T(8,128)(2,1)S(1)} all-to-all(bf16[8,9,32,128]{3,2,1,0:T(8,128)(2,1)S(1)} %bitcast.141), channel_id=1, replica_groups=mesh['wave'=4,'dom'=8] {'dom'}, dimensions={0} | all-to-all | bytes 1179648 | tf_op jit(solution)/shard_map/while/body/eval_jaxpr/all_to_all | solution.py:55
  303.9 10.6 %collective-permute-done.1 = bf16[8,9,32,128]{3,2,1,0:T(8,128)(2,1)S(1)} collective-permute-done((bf16[8,9,32,128]{3,2,1,0:T(8,128)(2,1)S(1)}, bf16[8,9,32,128]{3,2,1,0:T(8,128)(2,1)S(1)}, u32[]{:S(2)}, u32[]{:S(2)}) %collective-permute-start.1) | collective-permute-done | bytes 589856 | tf_op jit(solution)/shard_map/while/body/eval_jaxpr/ppermute | solution.py:15
  317.7 5.4 %copy.53 = bf16[12,32,625]{1,0,2:T(8,128)(2,1)S(1)} copy(f32[12,32,625]{2,1,0:T(8,128)} %get-tuple-element.813) | data formatting | bytes 1440000 | tf_op jit(solution)/shard_map/while/body/eval_jaxpr/cond | solution.py:92
  329.0 14.4 %all_to_all.34 = bf16[8,9,32,128]{3,2,1,0:T(8,128)(2,1)S(1)} all-to-all(bf16[8,9,32,128]{3,2,1,0:T(8,128)(2,1)S(1)} %bitcast.141), channel_id=1, replica_groups=mesh['wave'=4,'dom'=8] {'dom'}, dimensions={0} | all-to-all | bytes 1179648 | tf_op jit(solution)/shard_map/while/body/eval_jaxpr/all_to_all | solution.py:55
  344.7 29.7 %collective-permute-done.1 = bf16[8,9,32,128]{3,2,1,0:T(8,128)(2,1)S(1)} collective-permute-done((bf16[8,9,32,128]{3,2,1,0:T(8,128)(2,1)S(1)}, bf16[8,9,32,128]{3,2,1,0:T(8,128)(2,1)S(1)}, u32[]{:S(2)}, u32[]{:S(2)}) %collective-permute-start.1) | collective-permute-done | bytes 589856 | tf_op jit(solution)/shard_map/while/body/eval_jaxpr/ppermute | solution.py:15
  377.4 10.9 %conditional.7 = (f32[12,32,625]{2,1,0:T(8,128)}) conditional(s32[]{:T(128)} %convert_element_type.70, f32[12,32,625]{2,1,0:T(8,128)} %get-tuple-element.787, (bf16[8,9,32,128]{3,2,1,0:T(8,128)(2,1)S(1)}, s32[36]{0:T(128)S(1)}, bf16[12,3,128,625]{2,3,1,0:T(8,128)(2,1)}, f32[12,32,625]{2,1,0:T(8,128)}, bf16[12,625,625]{2,1,0:T(8,128)(2,1)}) %tuple.110), branch_computations={%region_5.5_spmd, %region_6.6_spmd} | conditional | flops 484801120 | bytes 19132258 | solution.py:92
  378.1 10.2 %fusion.5 = f32[12,32,625]{2,1,0:T(8,128)} fusion(bf16[12,625,625]{2,1,0:T(8,128)(2,1)} %get-tuple-element.500, f32[12,32,625]{2,1,0:T(8,128)} %get-tuple-element.496, bf16[12,3,32,128]{3,2,1,0:T(8,128)(2,1)S(1)} %bitcast.151, bf16[12,3,128,625]{2,3,1,0:T(8,128)(2,1)} %get-tuple-element.499), kind=kOutput, calls=%fused_computation.16 | convolution fusion | flops 484800000 | bytes 17349912 | tf_op jit(solution)/shard_map/while/body/eval_jaxpr/cond/branch_1_fun/eri,eij->erj/dot_general | solution.py:87
  388.3 5.4 %copy.53 = bf16[12,32,625]{1,0,2:T(8,128)(2,1)S(1)} copy(f32[12,32,625]{2,1,0:T(8,128)} %get-tuple-element.813) | data formatting | bytes 1440000 | tf_op jit(solution)/shard_map/while/body/eval_jaxpr/cond | solution.py:92
  399.6 16.5 %all_to_all.34 = bf16[8,9,32,128]{3,2,1,0:T(8,128)(2,1)S(1)} all-to-all(bf16[8,9,32,128]{3,2,1,0:T(8,128)(2,1)S(1)} %bitcast.141), channel_id=1, replica_groups=mesh['wave'=4,'dom'=8] {'dom'}, dimensions={0} | all-to-all | bytes 1179648 | tf_op jit(solution)/shard_map/while/body/eval_jaxpr/all_to_all | solution.py:55
  (173 shorter events, 104.2 us)
Async XLA Ops:
  0.6 14.3 %copy-start.1 = (s32[1,1,8,9]{3,2,1,0:T(8,128)S(1)}, s32[1,1,8,9]{3,2,1,0:T(8,128)}, u32[]{:S(2)}) copy-start(s32[1,1,8,9]{3,2,1,0:T(8,128)} %param.24) | copy-start | bytes 868
  2.9 38.5 %copy-start.3 = (s32[1,1,36]{2,1,0:T(1,128)S(1)}, s32[1,1,36]{2,1,0:T(1,128)}, u32[]{:S(2)}) copy-start(s32[1,1,36]{2,1,0:T(1,128)} %param.25) | copy-start | bytes 436
  8.3 36.3 %copy-start = (f32[1,1,12,32,625]{4,3,2,1,0:T(8,128)S(1)}, f32[1,1,12,32,625]{4,3,2,1,0:T(8,128)}, u32[]{:S(2)}) copy-start(f32[1,1,12,32,625]{4,3,2,1,0:T(8,128)} %param.17) | copy-start | bytes 2880004
  16.7 33.5 %copy-start.2 = (s32[1,1,8,9]{3,2,1,0:T(8,128)S(1)}, s32[1,1,8,9]{3,2,1,0:T(8,128)}, u32[]{:S(2)}) copy-start(s32[1,1,8,9]{3,2,1,0:T(8,128)} %param.22) | copy-start | bytes 868
  16.7 23.3 %all-to-all-start.2 = ((bf16[8,9,32,128]{3,2,1,0:T(8,128)(2,1)}), bf16[8,9,32,128]{3,2,1,0:T(8,128)(2,1)S(1)}, u32[]{:S(2)}, u32[]{:S(2)}) async-start(bf16[8,9,32,128]{3,2,1,0:T(8,128)(2,1)} %bitcast.18), calls=%async_computation.2 | async-start | bytes 1179648 | tf_op jit(solution)/shard_map/all_to_all | solution.py:55
  40.1 3.9 collective-permute-start.2
  90.7 2.9 collective-permute-start
  121.3 17.2 %collective-permute-start = (bf16[8,9,32,128]{3,2,1,0:T(8,128)(2,1)S(1)}, bf16[8,9,32,128]{3,2,1,0:T(8,128)(2,1)S(1)}, u32[]{:S(2)}, u32[]{:S(2)}) collective-permute-start(bf16[8,9,32,128]{3,2,1,0:T(8,128)(2,1)S(1)} %all_to_all.33), channel_id=1, source_target_pairs={{0,8},{8,16},{16,24},{1,9},{9,17},{17,25},{2,10},{10,18},{18,26},{... | collective-permute-start | bytes 1769480 | tf_op jit(solution)/shard_map/while/body/eval_jaxpr/ppermute | solution.py:15
  169.6 6.2 %collective-permute-start = (bf16[8,9,32,128]{3,2,1,0:T(8,128)(2,1)S(1)}, bf16[8,9,32,128]{3,2,1,0:T(8,128)(2,1)S(1)}, u32[]{:S(2)}, u32[]{:S(2)}) collective-permute-start(bf16[8,9,32,128]{3,2,1,0:T(8,128)(2,1)S(1)} %all_to_all.33), channel_id=1, source_target_pairs={{0,8},{8,16},{16,24},{1,9},{9,17},{17,25},{2,10},{10,18},{18,26},{... | collective-permute-start | bytes 1769480 | tf_op jit(solution)/shard_map/while/body/eval_jaxpr/ppermute | solution.py:15
  203.5 20.3 %collective-permute-start = (bf16[8,9,32,128]{3,2,1,0:T(8,128)(2,1)S(1)}, bf16[8,9,32,128]{3,2,1,0:T(8,128)(2,1)S(1)}, u32[]{:S(2)}, u32[]{:S(2)}) collective-permute-start(bf16[8,9,32,128]{3,2,1,0:T(8,128)(2,1)S(1)} %all_to_all.33), channel_id=1, source_target_pairs={{0,8},{8,16},{16,24},{1,9},{9,17},{17,25},{2,10},{10,18},{18,26},{... | collective-permute-start | bytes 1769480 | tf_op jit(solution)/shard_map/while/body/eval_jaxpr/ppermute | solution.py:15
  223.9 8.7 %copy-start.4 = (s32[1,1,36]{2,1,0:T(1,128)S(1)}, s32[1,1,36]{2,1,0:T(1,128)}, u32[]{:S(2)}) copy-start(s32[1,1,36]{2,1,0:T(1,128)} %param.25) | copy-start | bytes 436
  258.3 16.6 %collective-permute-start.1 = (bf16[8,9,32,128]{3,2,1,0:T(8,128)(2,1)S(1)}, bf16[8,9,32,128]{3,2,1,0:T(8,128)(2,1)S(1)}, u32[]{:S(2)}, u32[]{:S(2)}) collective-permute-start(bf16[8,9,32,128]{3,2,1,0:T(8,128)(2,1)S(1)} %all_to_all.34), channel_id=1, source_target_pairs={{8,0},{16,8},{24,16},{9,1},{17,9},{25,17},{10,2},{18,10},{26,18},{... | collective-permute-start | bytes 1769480 | tf_op jit(solution)/shard_map/while/body/eval_jaxpr/ppermute | solution.py:15
  302.6 11.9 %collective-permute-start.1 = (bf16[8,9,32,128]{3,2,1,0:T(8,128)(2,1)S(1)}, bf16[8,9,32,128]{3,2,1,0:T(8,128)(2,1)S(1)}, u32[]{:S(2)}, u32[]{:S(2)}) collective-permute-start(bf16[8,9,32,128]{3,2,1,0:T(8,128)(2,1)S(1)} %all_to_all.34), channel_id=1, source_target_pairs={{8,0},{16,8},{24,16},{9,1},{17,9},{25,17},{10,2},{18,10},{26,18},{... | collective-permute-start | bytes 1769480 | tf_op jit(solution)/shard_map/while/body/eval_jaxpr/ppermute | solution.py:15
  343.4 31.0 %collective-permute-start.1 = (bf16[8,9,32,128]{3,2,1,0:T(8,128)(2,1)S(1)}, bf16[8,9,32,128]{3,2,1,0:T(8,128)(2,1)S(1)}, u32[]{:S(2)}, u32[]{:S(2)}) collective-permute-start(bf16[8,9,32,128]{3,2,1,0:T(8,128)(2,1)S(1)} %all_to_all.34), channel_id=1, source_target_pairs={{8,0},{16,8},{24,16},{9,1},{17,9},{25,17},{10,2},{18,10},{26,18},{... | collective-permute-start | bytes 1769480 | tf_op jit(solution)/shard_map/while/body/eval_jaxpr/ppermute | solution.py:15
  416.0 3.9 collective-permute-start.1
where the time goes:
time: 428 us; the launch traced here: 422 us
  blocking collectives  122 us (29%)
  local copies, waits for them, and re-layouts  117 us (27%)
  waiting for transfers between devices  82.2 us (19%)
  starting transfers between devices  54 us (13%)
  matrix products  31.7 us (7%)
  other arithmetic  13.3 us (3%)
    ppermute x9, waiting for transfers between devices, shifted(): return lax.ppermute(array, axis, pairs)  66.3 us
    all_to_all x4, blocking collectives, route_down(): lax.all_to_all(buffer, 'dom', split_axis=0, concat_axis=0, tiled=True)  62.7 us
    all_to_all x4, blocking collectives, route_up(): lax.all_to_all(buffer, 'dom', split_axis=0, concat_axis=0, tiled=True)  59.7 us
    ppermute x9, starting transfers between devices, shifted(): return lax.ppermute(array, axis, pairs)  46.6 us
    cond x8, local copies, waits for them, and re-layouts, one_turn(): new_rows = lax.cond(active, fresh_rows, stale_rows)  43.4 us
    squeeze x24, local copies, waits for them, and re-layouts, face_traces(): stacked = jnp.stack(flat_faces, axis=-3)  29.6 us
    dot_general x2, matrix products, fresh_rows(): jnp.einsum('eri,eij->erj', residual, inverse, preferred_element_type=jnp....  20.3 us
    all_to_all x1, waiting for transfers between devices, route_up(): lax.all_to_all(buffer, 'dom', split_axis=0, concat_axis=0, tiled=True)  15.9 us
  transfers between devices with their start and end apart: 10, of which 10 were waited for; matrix products, arithmetic and copies ran while one was open for 0% of the time, Pallas kernels for 0%

commit v1 on v0

v1 whole, which is shorter than its diff:
```python
import functools

import jax
import jax.numpy as jnp
import numpy as np
from jax import lax
from jax.experimental import pallas as pl
from jax.experimental.pallas import tpu as pltpu
from jax.sharding import PartitionSpec as P

VARS = 5
NODES1 = 5
FACE = 125
FTR = 128
MESH = pl.DeviceIdType.MESH
F32 = jnp.float32
BF16 = jnp.bfloat16


def face_columns():
    columns = np.full((8, FTR), -1, np.int32)
    t = np.arange(FACE)
    var, i, j = t // 25, (t // 5) % 5, t % 5
    for side in range(2):
        edge = 0 if side == 0 else NODES1 - 1
        columns[3 * side + 0, :FACE] = var * 125 + edge * 25 + i * 5 + j
        columns[3 * side + 1, :FACE] = var * 125 + i * 25 + edge * 5 + j
        columns[3 * side + 2, :FACE] = var * 125 + i * 25 + j * 5 + edge
    return columns


def kernel(
    levels, parts,
    rhs_h, start_h, inv_h, cup_h, cdn_h, dpick, dslot, upick, uslot, cols,
    half_h, sol_h,
    rhs_v, work_v, half_v, inv_v, cup_v, cdn_v, mup_v, mdn_v, rb_v, sel_v, faces_v,
    send_old, send_up, send_low, recv_old, recv_up, recv_low,
    load_sem, inv_sem, cup_sem, cdn_sem, out_sem, ssem, rsem,
):
    wave = lax.axis_index("wave")
    dom = lax.axis_index("dom")
    elems, rows, block = rhs_v.shape
    slots = dpick.shape[1]
    nslot = parts * slots
    nface = 3 * elems
    first = wave == 0
    last = wave == levels - 1

    start_copy = pltpu.make_async_copy(start_h, work_v, load_sem.at[0])
    start_copy.start()
    rhs_copy = pltpu.make_async_copy(rhs_h, rhs_v, load_sem.at[1])
    rhs_copy.start()
    inv_copy = lambda e: pltpu.make_async_copy(inv_h.at[e], inv_v.at[e], inv_sem.at[e])
    cdn_copy = lambda e: pltpu.make_async_copy(cdn_h.at[e], cdn_v.at[e], cdn_sem.at[e])
    cup_copy = lambda e: pltpu.make_async_copy(cup_h.at[e], cup_v.at[e], cup_sem.at[e])
    for e in range(elems):
        inv_copy(e).start()
        cdn_copy(e).start()
    for e in range(elems):
        cup_copy(e).start()

    barrier = pltpu.get_barrier_semaphore()

    def greet(to):
        @pl.loop(0, parts)
        def _(d):
            pl.semaphore_signal(barrier, inc=1, device_id=(to, d), device_id_type=MESH)

    pl.when(wave > 0)(lambda: greet(wave - 1))
    pl.when(wave < levels - 1)(lambda: greet(wave + 1))

    zero = jnp.zeros((rows, FTR), BF16)
    faces_v[nface] = zero
    recv_old[nslot] = zero
    recv_up[nslot] = zero
    recv_low[nslot] = zero
    row_ids = lax.broadcasted_iota(jnp.int32, (block, FTR), 0)
    for q in range(6):
        hit = row_ids == jnp.broadcast_to(cols[q : q + 1, :], (block, FTR))
        sel_v[q // 3, :, (q % 3) * FTR : (q % 3 + 1) * FTR] = jnp.where(hit, 1.0, 0.0).astype(BF16)

    def traces(field, side):
        flat = field[...].reshape(elems * rows, block).astype(BF16)
        got = jnp.dot(flat, sel_v[side], preferred_element_type=F32).astype(BF16)
        for e in range(elems):
            for k in range(3):
                faces_v[3 * e + k] = got[e * rows : (e + 1) * rows, k * FTR : (k + 1) * FTR]

    def copy_to(phase, send, recv, to, d):
        return pltpu.make_async_remote_copy(
            src_ref=send.at[pl.ds(d * slots, slots)],
            dst_ref=recv.at[pl.ds(dom * slots, slots)],
            send_sem=ssem.at[phase, d],
            recv_sem=rsem.at[phase, dom],
            device_id=(to, d),
            device_id_type=MESH,
        )

    def send_all(phase, pick, send, recv, to):
        @pl.loop(0, parts)
        def _(i):
            d = lax.rem(dom + parts // 2 + i, parts)
            for j in range(slots):
                send[d * slots + j] = faces_v[pick[d, j]]
            copy_to(phase, send, recv, to, d).start()

    def finish_send(phase, send, recv, to):
        @pl.loop(0, parts)
        def _(d):
            copy_to(phase, send, recv, to, d).wait_send()

    def finish_recv(phase, send, recv, source):
        @pl.loop(0, parts)
        def _(s):
            pltpu.make_async_remote_copy(
                src_ref=send.at[pl.ds(s * slots, slots)],
                dst_ref=recv.at[pl.ds(s * slots, slots)],
                send_sem=ssem.at[phase, s],
                recv_sem=rsem.at[phase, s],
                device_id=(source, s),
                device_id_type=MESH,
            ).wait_recv()

    def near(recv, slot, e):
        return jnp.concatenate([recv[slot[3 * e + k]] for k in range(3)], axis=1)

    def fold(c_v, m_v, e):
        three = jnp.concatenate([c_v[e, k] for k in range(3)], axis=1)
        m_v[e] = lax.dot_general(
            three, inv_v[e], (((0,), (0,)), ((), ())), preferred_element_type=F32
        ).astype(BF16)

    start_copy.wait()
    traces(work_v, 0)

    sides = jnp.where(first, 0, 1) + jnp.where(last, 0, 1)
    pl.semaphore_wait(barrier, parts * sides)
    pl.when(wave > 0)(lambda: send_all(0, upick, send_old, recv_old, wave - 1))

    rhs_copy.wait()

    @pl.loop(0, elems)
    def _(e):
        inv_copy(e).wait()
        cdn_copy(e).wait()
        rb_v[e] = jnp.dot(rhs_v[e].astype(BF16), inv_v[e], preferred_element_type=F32)
        half_v[e] = rb_v[e]

        @pl.when(wave < levels - 1)
        def _():
            fold(cdn_v, mdn_v, e)

    @pl.when(wave < levels - 1)
    def _():
        finish_recv(0, send_old, recv_old, wave + 1)

        @pl.loop(0, elems)
        def _(e):
            half_v[e] = rb_v[e] - jnp.dot(near(recv_old, uslot, e), mdn_v[e], preferred_element_type=F32)

    @pl.loop(0, elems)
    def _(e):
        cup_copy(e).wait()

    @pl.when(wave > 0)
    def _():
        @pl.loop(0, elems)
        def _(e):
            fold(cup_v, mup_v, e)

        finish_recv(1, send_up, recv_up, wave - 1)

        @pl.loop(0, elems)
        def _(e):
            term = jnp.dot(near(recv_up, dslot, e), mup_v[e], preferred_element_type=F32)
            half_v[e] = half_v[e] - term
            rb_v[e] = rb_v[e] - term

    @pl.when(wave < levels - 1)
    def _():
        traces(half_v, 1)
        send_all(1, dpick, send_up, recv_up, wave + 1)

    half_copy = pltpu.make_async_copy(half_v, half_h, out_sem.at[0])
    half_copy.start()

    @pl.when(last)
    def _():
        work_v[...] = half_v[...]

    @pl.when(wave < levels - 1)
    def _():
        finish_recv(2, send_low, recv_low, wave + 1)

        @pl.loop(0, elems)
        def _(e):
            work_v[e] = rb_v[e] - jnp.dot(near(recv_low, uslot, e), mdn_v[e], preferred_element_type=F32)

    @pl.when(wave > 0)
    def _():
        traces(work_v, 0)
        send_all(2, upick, send_low, recv_low, wave - 1)

    sol_copy = pltpu.make_async_copy(work_v, sol_h, out_sem.at[1])
    sol_copy.start()

    @pl.when(wave > 0)
    def _():
        finish_send(0, send_old, recv_old, wave - 1)
        finish_send(2, send_low, recv_low, wave - 1)

    @pl.when(wave < levels - 1)
    def _():
        finish_send(1, send_up, recv_up, wave + 1)

    half_copy.wait()
    sol_copy.wait()


def local(rhs, start, block_inv, coup_up, coup_down, down_pick, down_slot, up_pick, up_slot):
    levels, parts = lax.axis_size("wave"), lax.axis_size("dom")
    elems, rows, block = rhs.shape[2:]
    slots = down_pick.shape[-1]
    nslot = parts * slots
    field = jax.ShapeDtypeStruct((elems, rows, block), F32)
    anywhere = pl.BlockSpec(memory_space=pl.ANY)
    scalar = pl.BlockSpec(memory_space=pltpu.SMEM)
    fold_shape = (elems, 3 * FTR, block)
    coup_shape = (elems, 3, block, FTR)
    half, final = pl.pallas_call(
        functools.partial(kernel, levels, parts),
        out_shape=(field, field),
        in_specs=[anywhere] * 5 + [scalar] * 4 + [pl.BlockSpec(memory_space=pltpu.VMEM)],
        out_specs=(anywhere, anywhere),
        scratch_shapes=[
            pltpu.VMEM((elems, rows, block), F32),
            pltpu.VMEM((elems, rows, block), F32),
            pltpu.VMEM((elems, rows, block), F32),
            pltpu.VMEM((elems, block, block), BF16),
            pltpu.VMEM(coup_shape, BF16),
            pltpu.VMEM(coup_shape, BF16),
            pltpu.VMEM(fold_shape, BF16),
            pltpu.VMEM(fold_shape, BF16),
            pltpu.VMEM((elems, rows, block), F32),
            pltpu.VMEM((2, block, 3 * FTR), BF16),
            pltpu.VMEM((3 * elems + 1, rows, FTR), BF16),
        ]
        + [pltpu.VMEM((nslot, rows, FTR), BF16)] * 3
        + [pltpu.VMEM((nslot + 1, rows, FTR), BF16)] * 3
        + [
            pltpu.SemaphoreType.DMA((2,)),
            pltpu.SemaphoreType.DMA((elems,)),
            pltpu.SemaphoreType.DMA((elems,)),
            pltpu.SemaphoreType.DMA((elems,)),
            pltpu.SemaphoreType.DMA((2,)),
            pltpu.SemaphoreType.DMA((3, parts)),
            pltpu.SemaphoreType.DMA((3, parts)),
        ],
        compiler_params=pltpu.CompilerParams(
            collective_id=0, has_side_effects=True, vmem_limit_bytes=62 * 1024 * 1024
        ),
    )(
        rhs[0, 0],
        start[0, 0],
        block_inv[0, 0],
        jnp.swapaxes(coup_up[0, 0], -1, -2),
        jnp.swapaxes(coup_down[0, 0], -1, -2),
        down_pick[0, 0],
        down_slot[0, 0],
        up_pick[0, 0],
        up_slot[0, 0],
        jnp.asarray(face_columns()),
    )
    return (half[None, None], final[None, None])


def solution(mesh):
    placed = (
        P("wave", "dom", None, None, None),
        P("wave", "dom", None, None, None),
        P("wave", "dom", None, None, None),
        P("wave", "dom", None, None, None, None),
        P("wave", "dom", None, None, None, None),
        P("wave", "dom", None, None),
        P("wave", "dom", None),
        P("wave", "dom", None, None),
        P("wave", "dom", None),
    )
    return jax.shard_map(
        local,
        mesh=mesh,
        in_specs=placed,
        out_specs=(P("wave", "dom", None, None, None), P("wave", "dom", None, None, None)),
        check_vma=False,
    )
```

time: 428 us -> 104 us (0.24); the launches traced: 422 us -> 104 us
  blocking collectives: 122 us -> 0 us
  local copies, waits for them, and re-layouts: 117 us -> 4.42 us
  Pallas kernels: 0 us -> 98.5 us
  waiting for transfers between devices: 82.2 us -> 0 us
  starting transfers between devices: 54 us -> 0 us
  matrix products: 31.7 us -> 0 us
  other arithmetic: 13.3 us -> 0 us
    all_to_all x8 -> x0, blocking collectives: 122 us -> none  [the longest x4 62.7 us: route_down(): lax.all_to_all(buffer, 'dom', split_axis=0, concat_axis=0, tiled=True)]
    pallas_call x0 -> x1, Pallas kernels: none -> 98.5 us  [local(): pl.pallas_call(functools.partial(kernel, levels, parts), out_shape=(field...]
    ppermute x9 -> x0, waiting for transfers between devices: 66.3 us -> none  [shifted(): return lax.ppermute(array, axis, pairs)]
    ppermute x9 -> x0, starting transfers between devices: 46.6 us -> none  [shifted(): return lax.ppermute(array, axis, pairs)]
    cond x8 -> x0, local copies, waits for them, and re-layouts: 43.4 us -> none  [one_turn(): new_rows = lax.cond(active, fresh_rows, stale_rows)]
    dot_general x4 -> x0, matrix products: 31.7 us -> none  [the longest x2 20.3 us: fresh_rows(): jnp.einsum('eri,eij->erj', residual, inverse, preferred_element_type=jnp....]
    squeeze x24 -> x0, local copies, waits for them, and re-layouts: 29.6 us -> none  [face_traces(): stacked = jnp.stack(flat_faces, axis=-3)]
    slice x27 -> x0, local copies, waits for them, and re-layouts: 19.2 us -> none  [the longest x9 7.49 us: face_traces(): cube[..., :, edge_at, :]]
  transfers between devices with their start and end apart: 10 -> 0, of which waited for: 10 -> 0; matrix products, arithmetic and copies ran while one was open for 0% -> 0% of each run, Pallas kernels for 0% -> 0%
where the time goes in v1:
time: 104 us
  Pallas kernels  98.5 us (95%)
  local copies, waits for them, and re-layouts  4.42 us (4%)
    pallas_call x1, Pallas kernels, local(): pl.pallas_call(functools.partial(kernel, levels, parts), out_shape=(field...  98.5 us
    unnamed x2, local copies, waits for them, and re-layouts  4.42 us

profile of v1, /device:TPU:0, one launch (start us, length us, event | category | flops | bytes accessed | tf_op | source)
XLA Modules:
  0.0 103.6 jit_solution(4619472060674048448)
XLA Ops:
  0.6 98.5 %shard_map.113 = (f32[12,32,625]{2,1,0:T(8,128)}, f32[12,32,625]{2,1,0:T(8,128)}) custom-call(f32[12,32,625]{2,1,0:T(8,128)} %bitcast.18, f32[12,32,625]{2,1,0:T(8,128)} %bitcast.19, bf16[12,625,625]{2,1,0:T(8,128)(2,1)} %bitcast.15, bf16[12,3,625,128]{3,2,1,0:T(8,128)(2,1)} %bitcast.16, bf16[12,3,625,128]{3,2,1,0:T(8,128)(2,1)} %bitcast.17, ...), custom_call_target="tpu_custom_call" | custom-call | tf_op jit(solution)/shard_map/pallas_call | solution.py:230
  99.2 2.2 %copy.14 = f32[1,1,12,32,625]{4,3,2,1,0:T(8,128)} copy(f32[1,1,12,32,625]{4,3,2,1,0:T(8,128)} %bitcast.21) | data formatting | bytes 1920000
  101.4 2.2 %copy.15 = f32[1,1,12,32,625]{4,3,2,1,0:T(8,128)} copy(f32[1,1,12,32,625]{4,3,2,1,0:T(8,128)} %bitcast.20) | data formatting | bytes 1920000
